TPU v7x, 32 devices: a whole 2x2x4 slice. The times are simulated.
32 devices in a mesh: expert: 8 (over y, x, core), dp: 4 (over z).
Axes of the slice: x: 2, y: 2, z: 4, core: 2. Of those that a mesh axis runs over, the one named last changes fastest.
Arguments:
- tokens: bfloat16 [4096, 2048], P(('expert', 'dp')), may hold values from -6 to 6
- expert_ids: int32 [4096, 8], P(('expert', 'dp')), may hold values from 0 to 15, all different within a row; in each aligned block of 128 rows (0 to 127, 128 to 255, ...) at most 72 rows name the same one
- router: bfloat16 [2048, 16], replicated, may hold values from -0.25 to 0.25
- w_gate: bfloat16 [16, 2048, 640], P('expert'), may hold values from -0.125 to 0.125
- w_up: bfloat16 [16, 2048, 640], P('expert'), may hold values from -0.125 to 0.125
- w_down: bfloat16 [16, 640, 2048], P('expert'), may hold values from -1 to 1
- out_grad: bfloat16 [4096, 2048], P(('expert', 'dp')), may hold values from -6 to 6
Outputs:
- mixed: bfloat16 [4096, 2048], P(('expert', 'dp'))
- token_grad: bfloat16 [4096, 2048], P(('expert', 'dp'))
- router_grad: float32 [2048, 16], replicated
- gate_grad: bfloat16 [16, 2048, 640], P('expert', 'dp')
- up_grad: bfloat16 [16, 2048, 640], P('expert', 'dp')
- down_grad: bfloat16 [16, 640, 2048], P('expert', None, 'dp')
Inputs may be any that keep to these rules, and one draw needn't show every extreme that they name: `expert_ids`: each row names 8 different experts; within the 128 rows of one device no expert is named more than 72 times.
All inputs are finite; a program needn't handle non-finite values.
Results may differ from a plain program's by a relative error of at most 0.008.
Values may be sent and summed in bfloat16 or wider, within the bound.
No kernel may reach another device: no remote copies, remote signals or barrier semaphores. Data moves between devices by JAX's collectives and lax.ppermute only.
A program may use at most 256 MiB of HBM per device.

v0:
```python
import jax
import jax.numpy as jnp
from jax import lax
from jax.sharding import PartitionSpec as P


def flat_rows(array):
    return array.reshape(array.shape[0], array.shape[1] * array.shape[2], array.shape[3])


def body(tokens, expert_ids, router, w_gate, w_up, w_down, out_grad):
    f32 = jnp.float32
    bf16 = jnp.bfloat16
    tok_dev, width = tokens.shape
    top = expert_ids.shape[1]
    n_experts = router.shape[1]
    local_experts = w_gate.shape[0]
    groups = lax.axis_size("expert")
    capacity = (tok_dev * top * 9 + 8 * n_experts - 1) // (8 * n_experts)
    n_assign = tok_dev * top
    flat_ids = expert_ids.reshape(-1)
    ladder = jnp.arange(n_experts, dtype=jnp.int32)
    onehot = (flat_ids[:, None] == ladder[None, :]).astype(jnp.int32)
    rank = jnp.sum((jnp.cumsum(onehot, axis=0) - onehot) * onehot, axis=1)
    owner = flat_ids // local_experts
    within = flat_ids % local_experts
    dest = (within * groups + owner) * capacity + rank
    slot_src = jnp.full((n_experts * capacity,), n_assign, jnp.int32)
    slot_src = slot_src.at[dest].set(jnp.arange(n_assign, dtype=jnp.int32))
    live = slot_src < n_assign
    slot_tok = jnp.where(live, slot_src // top, 0)
    logits = jnp.dot(tokens, router, preferred_element_type=f32)
    scores = jax.nn.sigmoid(logits)
    chosen = jnp.take_along_axis(scores, expert_ids, axis=1)
    total = jnp.sum(chosen, axis=1, keepdims=True)
    gates = chosen / total
    gate_slots = jnp.where(live, gates.reshape(-1)[jnp.minimum(slot_src, n_assign - 1)], 0.0)
    send = jnp.where(live[:, None], tokens[slot_tok], jnp.zeros((), bf16))
    send = send.reshape(local_experts, groups, capacity, width)
    piece = lax.all_to_all(send, "expert", split_axis=1, concat_axis=1, tiled=True)
    shape = piece.shape
    rows = flat_rows(piece)
    pre_gate = jnp.einsum("jrd,jdf->jrf", rows, w_gate, preferred_element_type=f32)
    pre_up = jnp.einsum("jrd,jdf->jrf", rows, w_up, preferred_element_type=f32)
    hidden = (pre_gate * jax.nn.sigmoid(pre_gate) * pre_up).astype(bf16)
    expert_out = jnp.einsum("jrf,jfd->jrd", hidden, w_down, preferred_element_type=f32).astype(bf16)
    hid_shape = (shape[0], shape[1], shape[2], hidden.shape[2])
    expert_out = expert_out.reshape(shape)
    hidden = hidden.reshape(hid_shape)
    results = (expert_out, hidden, piece, pre_gate.reshape(hid_shape), pre_up.reshape(hid_shape))
    expert_out = results[0]
    hidden = flat_rows(results[1])
    back = lax.all_to_all(expert_out, "expert", split_axis=1, concat_axis=1, tiled=True).reshape(
        n_experts * capacity, width
    )
    picked = back[dest].reshape(tok_dev, top, width)
    mixed = jnp.einsum("tk,tkd->td", gates, picked.astype(f32)).astype(bf16)
    gate_sens = jnp.einsum("tkd,td->tk", picked, out_grad, preferred_element_type=f32)
    grad_rows = (gate_slots[:, None] * out_grad[slot_tok].astype(f32)).astype(bf16)
    grad_send = jnp.where(live[:, None], grad_rows, jnp.zeros((), bf16))
    grad_send = grad_send.reshape(local_experts, groups, capacity, width)
    grad_in4 = lax.all_to_all(grad_send, "expert", split_axis=1, concat_axis=1, tiled=True)
    grad_in = flat_rows(grad_in4)
    pre_gate = flat_rows(results[3])
    pre_up = flat_rows(results[4])
    hidden_grad = jnp.einsum("jrd,jfd->jrf", grad_in, w_down, preferred_element_type=f32)
    sig = jax.nn.sigmoid(pre_gate)
    silu_val = pre_gate * sig
    gate_term = (hidden_grad * pre_up * sig * (1.0 + pre_gate * (1.0 - sig))).astype(bf16)
    up_term = (hidden_grad * silu_val).astype(bf16)
    input_grad = (
        jnp.einsum("jrf,jdf->jrd", gate_term, w_gate, preferred_element_type=f32)
        + jnp.einsum("jrf,jdf->jrd", up_term, w_up, preferred_element_type=f32)
    ).astype(bf16)
    input_grad = input_grad.reshape(grad_in4.shape)
    returned = lax.all_to_all(
        input_grad, "expert", split_axis=1, concat_axis=1, tiled=True
    ).reshape(n_experts * capacity, width)
    moe_grad = jnp.sum(returned[dest].reshape(tok_dev, top, width).astype(f32), axis=1)
    chosen_grad = (gate_sens - jnp.sum(gate_sens * gates, axis=1, keepdims=True)) / total
    sel_grad = chosen_grad * chosen * (1.0 - chosen)
    pick = (expert_ids[:, :, None] == ladder[None, None, :]).astype(f32)
    logit_grad = jnp.einsum("tk,tke->te", sel_grad, pick).astype(bf16)
    token_grad = (moe_grad + jnp.dot(logit_grad, router.T, preferred_element_type=f32)).astype(bf16)
    router_grad = lax.psum(
        jnp.dot(tokens.T, logit_grad, preferred_element_type=f32), ("expert", "dp")
    )
    hidden_width = hidden.shape[2]
    arrived4 = results[2]
    columns = (
        lax.all_to_all(arrived4, "dp", split_axis=3, concat_axis=1, tiled=True),
        lax.all_to_all(grad_in4, "dp", split_axis=3, concat_axis=1, tiled=True),
    )
    hid_shape = (local_experts, groups, capacity, hidden_width)
    hiddens = (
        lax.all_gather(gate_term.reshape(hid_shape), "dp", axis=1, tiled=True),
        lax.all_gather(up_term.reshape(hid_shape), "dp", axis=1, tiled=True),
        lax.all_gather(results[1], "dp", axis=1, tiled=True),
    )
    x_cols = flat_rows(columns[0])
    g_cols = flat_rows(columns[1])
    gate_grad = jnp.einsum(
        "jrd,jrf->jdf", x_cols, flat_rows(hiddens[0]), preferred_element_type=f32
    ).astype(bf16)
    up_grad = jnp.einsum(
        "jrd,jrf->jdf", x_cols, flat_rows(hiddens[1]), preferred_element_type=f32
    ).astype(bf16)
    down_grad = jnp.einsum(
        "jrf,jrd->jfd", flat_rows(hiddens[2]), g_cols, preferred_element_type=f32
    ).astype(bf16)
    return (mixed, token_grad, router_grad, gate_grad, up_grad, down_grad)


def solution(mesh):
    placed = (
        P(("expert", "dp"), None),
        P(("expert", "dp"), None),
        P(),
        P("expert", None, None),
        P("expert", None, None),
        P("expert", None, None),
        P(("expert", "dp"), None),
    )
    return jax.shard_map(
        body,
        mesh=mesh,
        in_specs=placed,
        out_specs=(
            P(("expert", "dp"), None),
            P(("expert", "dp"), None),
            P(),
            P("expert", "dp", None),
            P("expert", "dp", None),
            P("expert", None, "dp"),
        ),
        check_vma=False,
    )
```

profile of v0, /device:TPU:0, one launch (start us, length us, event | category | flops | bytes accessed | tf_op | source)
XLA Modules:
  0.0 936.1 jit_solution(13658574191496700082)
XLA Ops:
  8.0 0.9 copy.108
  9.2 4.5 reduce-window.6
  13.8 0.1 copy.111
  14.2 4.3 scatter_custom_fusion
  18.7 6.0 gather_fusion
  24.7 2.7 copy_select_fusion
  27.4 59.9 %all_to_all.50 = bf16[2,8,72,2048]{3,2,0,1:T(8,128)(2,1)S(1)} all-to-all(bf16[2,8,72,2048]{3,2,0,1:T(8,128)(2,1)S(1)} %copy_select_fusion), channel_id=1, replica_groups=mesh['expert'=8,'dp'=4] {'expert'}, dimensions={1} | all-to-all | bytes 9437184 | tf_op jit(solution)/shard_map/all_to_all | solution.py:40
  87.3 0.7 copy.115
  88.1 1.7 copy-done.3
  89.8 3.8 fusion.33
  93.6 5.7 multiply_convert_fusion.2
  99.3 4.1 convolution_convert_fusion
  103.5 2.5 copy.116
  106.0 4.7 all-to-all-start.1
  110.7 0.5 all-gather.8.cloned.1.call-start
  111.2 0.2 all-gather.8.cloned.1.call-update
  111.4 0.1 copy.106
  111.7 0.2 fusion.10
  111.9 7.0 gather_fusion.5
  119.1 5.9 gather_fusion.3
  125.1 40.4 %all-to-all-done.1 = bf16[2,8,72,2048]{3,2,0,1:T(8,128)(2,1)} async-done(((bf16[2,8,72,2048]{3,2,0,1:T(8,128)(2,1)}), bf16[2,8,72,2048]{3,2,0,1:T(8,128)(2,1)}, u32[]{:S(2)}, u32[]{:S(2)}) %all-to-all-start.1) | async-done | bytes 4718624 | tf_op jit(solution)/shard_map/all_to_all | solution.py:53
  165.4 5.2 copy.117
  170.6 11.8 %gather_fusion.1 = bf16[1024,2048]{1,0:T(8,128)(2,1)} fusion(bf16[1152,2048]{1,0:T(8,128)(2,1)} %bitcast.104, s32[1024]{0:T(1024)S(1)} %broadcast_clamp_fusion), kind=kCustom, calls=%fused_computation.1 | custom fusion | bytes 8392704 | tf_op jit(solution)/shard_map/gather | solution.py:56
  182.4 4.9 fusion.2
  187.6 4.6 gather_fusion.2
  192.3 4.4 fusion.1
  196.7 4.6 all-to-all-start.2
  201.3 11.7 %copy.125 = bf16[2,8,72,2048]{2,1,0,3:T(8,128)(2,1)} copy(bf16[2,8,72,2048]{3,2,0,1:T(8,128)(2,1)} %copy-done.3) | data formatting | bytes 9437184 | tf_op jit(solution)/shard_map/all_to_all | solution.py:40
  213.0 43.1 %all-to-all-done.2 = bf16[2,8,72,2048]{3,2,0,1:T(8,128)(2,1)} async-done(((bf16[2,8,72,2048]{3,2,0,1:T(8,128)(2,1)}), bf16[2,8,72,2048]{3,2,0,1:T(8,128)(2,1)}, u32[]{:S(2)}, u32[]{:S(2)}) %all-to-all-start.2) | async-done | bytes 4718624 | tf_op jit(solution)/shard_map/all_to_all | solution.py:62
  256.1 5.6 all-to-all-start.4
  261.7 0.2 all-gather.4.cloned.1.call-start
  261.9 2.9 copy.121
  264.8 0.4 copy-done.11
  265.2 0.9 copy-done.12
  266.1 8.5 multiply_convert_fusion
  274.6 11.3 %fusion.34 = f32[2,576,2048]{2,1,0:T(8,128)} fusion(bf16[2,576,640]{2,1,0:T(8,128)(2,1)} %get-tuple-element.11, bf16[2,2048,640]{2,1,0:T(8,128)(2,1)} %param.10), kind=kOutput, calls=%fused_computation.86 | convolution fusion | flops 3019898880 | bytes 16154624 | tf_op jit(solution)/shard_map/jrf,jdf->jrd/dot_general | solution.py:72
  285.9 8.1 add_convert_fusion
  294.0 2.5 copy.122
  296.5 240.4 %all-to-all-done.4 = bf16[2,8,72,2048]{2,1,0,3:T(8,128)(2,1)} async-done(((bf16[2,8,72,2048]{2,1,0,3:T(8,128)(2,1)}), bf16[2,8,72,2048]{2,1,0,3:T(8,128)(2,1)}, u32[]{:S(2)}, u32[]{:S(2)}) %all-to-all-start.4) | async-done | bytes 4718624 | tf_op jit(solution)/shard_map/all_to_all | solution.py:91
  536.9 5.0 all-to-all-start.3
  541.9 0.7 all-gather.6.cloned.1.call-update
  542.6 11.8 %copy.130 = bf16[2,8,72,2048]{2,1,0,3:T(8,128)(2,1)} copy(bf16[2,8,72,2048]{3,2,0,1:T(8,128)(2,1)} %all-to-all-done.2) | data formatting | bytes 9437184 | tf_op jit(solution)/shard_map/all_to_all | solution.py:62
  554.4 42.3 %all-to-all-done.3 = bf16[2,8,72,2048]{3,2,0,1:T(8,128)(2,1)} async-done(((bf16[2,8,72,2048]{3,2,0,1:T(8,128)(2,1)}), bf16[2,8,72,2048]{3,2,0,1:T(8,128)(2,1)}, u32[]{:S(2)}, u32[]{:S(2)}) %all-to-all-start.3) | async-done | bytes 4718624 | tf_op jit(solution)/shard_map/all_to_all | solution.py:76
  596.7 5.6 all-to-all-start.5
  602.3 0.3 all-reduce.2.cloned.1.call-start
  602.6 0.1 copy.133
  602.8 3.4 fusion.4
  606.2 1.1 copy.154
  607.3 0.1 copy.137
  607.4 0.3 fusion.12
  607.8 0.9 convolution_bitcast_fusion
  608.7 10.7 %copy.142 = bf16[2,8,72,4,512]{4,3,2,1,0:T(4,128)(2,1)} copy(bf16[2,8,72,4,512]{2,1,0,4,3:T(8,128)(2,1)} %bitcast.23) | data formatting | bytes 9437184 | tf_op jit(solution)/shard_map/all_to_all | solution.py:91
  619.4 5.5 copy.127
  624.9 5.3 copy.123
  630.2 11.8 %gather_fusion.4 = bf16[1024,2048]{1,0:T(8,128)(2,1)} fusion(bf16[1152,2048]{1,0:T(8,128)(2,1)} %bitcast.103, s32[1024]{0:T(1024)S(1)} %broadcast_clamp_fusion), kind=kCustom, calls=%fused_computation.4 | custom fusion | bytes 8392704 | tf_op jit(solution)/shard_map/gather | solution.py:79
  641.9 5.0 convert_reduce_fusion
  647.0 1.1 fusion.7
  648.0 185.0 %all-to-all-done.5 = bf16[2,8,72,2048]{2,1,0,3:T(8,128)(2,1)} async-done(((bf16[2,8,72,2048]{2,1,0,3:T(8,128)(2,1)}), bf16[2,8,72,2048]{2,1,0,3:T(8,128)(2,1)}, u32[]{:S(2)}, u32[]{:S(2)}) %all-to-all-start.5) | async-done | bytes 4718624 | tf_op jit(solution)/shard_map/all_to_all | solution.py:92
  833.0 13.3 %copy.131 = bf16[2,8,72,4,512]{4,2,1,3,0:T(8,128)(2,1)} copy(bf16[2,8,72,4,512]{2,1,0,4,3:T(8,128)(2,1)} %bitcast.32) | data formatting | bytes 9437184 | tf_op jit(solution)/shard_map/all_to_all | solution.py:92
  846.4 8.4 convolution_convert_fusion.1
  854.8 9.1 convolution_convert_fusion.3
  863.9 9.2 convolution_convert_fusion.2
  873.1 53.9 %all-reduce.2.cloned.1.call-done = f32[2048,16]{0,1:T(8,128)} async-done(((f32[2048,16]{0,1:T(8,128)}), f32[2048,16]{0,1:T(8,128)}) %all-reduce.2.cloned.1.call-update) | async-done | bytes 131088 | tf_op jit(solution)/shard_map/psum | solution.py:85
  927.0 1.6 copy.156
  (74 shorter events, 1.6 us)
Async XLA Ops:
  8.0 111.1 %copy-start = (bf16[128,2048]{1,0:T(8,128)(2,1)S(1)}, bf16[128,2048]{1,0:T(8,128)(2,1)}, u32[]{:S(2)}) copy-start(bf16[128,2048]{1,0:T(8,128)(2,1)} %param.13) | copy-start | bytes 1572868
  8.0 10.7 %copy-start.2 = (bf16[128,2048]{1,0:T(8,128)(2,1)S(1)}, bf16[128,2048]{1,0:T(8,128)(2,1)}, u32[]{:S(2)}) copy-start(bf16[128,2048]{1,0:T(8,128)(2,1)} %param.7) | copy-start | bytes 1572868
  8.9 15.8 %copy-start.6 = (s32[128,8]{1,0:T(8,128)}, s32[128,8]{1,0:T(8,128)S(1)}, u32[]{:S(2)}) copy-start(s32[128,8]{1,0:T(8,128)S(1)} %copy.108) | copy-start | bytes 12292
  27.4 62.3 %slice-start.2 = ((s8[5242880]{0:T(1024)(128)(4,1)}), s8[4194304]{0:T(1024)(128)(4,1)S(1)}, s32[]{:S(2)}) async-start(s8[5242880]{0:T(1024)(128)(4,1)} %bitcast.133), calls=%async_computation.12 | async-start | bytes 8388608
  87.3 2.4 copy-start.3
  87.3 2.4 slice-start.3
  87.3 6.3 slice-start.4
  89.7 3.9 slice-start.5
  89.7 9.6 %slice-start = ((s8[5242880]{0:T(1024)(128)(4,1)}), s8[4194304]{0:T(1024)(128)(4,1)S(1)}, s32[]{:S(2)}) async-start(s8[5242880]{0:T(1024)(128)(4,1)} %bitcast.131), calls=%async_computation.10 | async-start | bytes 8388608
  93.6 5.7 copy-start.10
  93.6 5.7 slice-start.1
  99.3 4.1 copy-start.4
  106.0 5.5 copy-start.9
  106.0 5.7 copy-start.8
  106.0 59.5 %all-to-all-start.1 = ((bf16[2,8,72,2048]{3,2,0,1:T(8,128)(2,1)}), bf16[2,8,72,2048]{3,2,0,1:T(8,128)(2,1)}, u32[]{:S(2)}, u32[]{:S(2)}) async-start(bf16[2,8,72,2048]{3,2,0,1:T(8,128)(2,1)} %copy.116), calls=%async_computation.1 | async-start | bytes 9437184 | tf_op jit(solution)/shard_map/all_to_all | solution.py:53
  110.7 735.7 %all-gather.8.cloned.1.call-start = ((), (), s32[]{:S(2)}) async-start(), calls=%async_computation.9 | async-start | bytes 7372800 | tf_op jit(solution)/shard_map/all_gather | solution.py:98
  196.7 59.4 %all-to-all-start.2 = ((bf16[2,8,72,2048]{3,2,0,1:T(8,128)(2,1)}), bf16[2,8,72,2048]{3,2,0,1:T(8,128)(2,1)}, u32[]{:S(2)}, u32[]{:S(2)}) async-start(bf16[2,8,72,2048]{3,2,0,1:T(8,128)(2,1)} %fusion.1), calls=%async_computation.2 | async-start | bytes 9437184 | tf_op jit(solution)/shard_map/all_to_all | solution.py:62
  256.1 280.8 %all-to-all-start.4 = ((bf16[2,8,72,2048]{2,1,0,3:T(8,128)(2,1)}), bf16[2,8,72,2048]{2,1,0,3:T(8,128)(2,1)}, u32[]{:S(2)}, u32[]{:S(2)}) async-start(bf16[2,8,72,2048]{2,1,0,3:T(8,128)(2,1)} %copy.125), calls=%async_computation.4 | async-start | bytes 16777216 | tf_op jit(solution)/shard_map/all_to_all | solution.py:91
  261.7 593.1 %all-gather.4.cloned.1.call-start = ((), (), s32[]{:S(2)}) async-start(), calls=%async_computation.7 | async-start | bytes 7372800 | tf_op jit(solution)/shard_map/all_gather | solution.py:96
  261.9 3.3 copy-start.11
  261.9 4.1 copy-start.12
  274.5 11.3 %copy-start.5 = (bf16[2,576,640]{2,1,0:T(8,128)(2,1)}, bf16[2,576,640]{2,1,0:T(8,128)(2,1)S(1)}, u32[]{:S(2)}) copy-start(bf16[2,576,640]{2,1,0:T(8,128)(2,1)S(1)} %get-tuple-element.10) | copy-start | bytes 4423684
  536.9 59.8 %all-to-all-start.3 = ((bf16[2,8,72,2048]{3,2,0,1:T(8,128)(2,1)}), bf16[2,8,72,2048]{3,2,0,1:T(8,128)(2,1)}, u32[]{:S(2)}, u32[]{:S(2)}) async-start(bf16[2,8,72,2048]{3,2,0,1:T(8,128)(2,1)} %copy.122), calls=%async_computation.3 | async-start | bytes 9437184 | tf_op jit(solution)/shard_map/all_to_all | solution.py:76
  541.8 322.1 %all-gather.6.cloned.1.call-start = ((), (), s32[]{:S(2)}) async-start(), calls=%async_computation.8 | async-start | bytes 7372800 | tf_op jit(solution)/shard_map/all_gather | solution.py:97
  596.7 236.3 %all-to-all-start.5 = ((bf16[2,8,72,2048]{2,1,0,3:T(8,128)(2,1)}), bf16[2,8,72,2048]{2,1,0,3:T(8,128)(2,1)}, u32[]{:S(2)}, u32[]{:S(2)}) async-start(bf16[2,8,72,2048]{2,1,0,3:T(8,128)(2,1)} %copy.130), calls=%async_computation.5 | async-start | bytes 16777216 | tf_op jit(solution)/shard_map/all_to_all | solution.py:92
  602.3 5.1 copy-start.7
  602.3 324.6 %all-reduce.2.cloned.1.call-start = ((), (), s32[]{:S(2)}) async-start(), calls=%async_computation.6 | async-start | bytes 262144 | tf_op jit(solution)/shard_map/psum | solution.py:85
  863.9 64.6 %copy-start.1 = (bf16[128,2048]{1,0:T(8,128)(2,1)S(1)}, bf16[128,2048]{1,0:T(8,128)(2,1)}, u32[]{:S(2)}) copy-start(bf16[128,2048]{1,0:T(8,128)(2,1)} %param.13) | copy-start | bytes 1572868
Sparse Core Ops, SparseCore 0:
  113.1 110.4 all-gather.7
  274.7 221.0 all-gather.3
  544.3 178.8 all-gather.5
Sparse Core Ops, SparseCore 1:
  608.9 318.0 all-reduce.1
where the time goes:
time: 946 us; the launch traced here: 936 us
  waiting for transfers between devices  606 us (64%)
  local copies, waits for them, and re-layouts  132 us (14%)
  matrix products  79 us (8%)
  blocking collectives  59.9 us (6%)
  starting transfers between devices  26.6 us (3%)
  other arithmetic  17 us (2%)
  between operations  16.1 us (2%)
    all_to_all x1, waiting for transfers between devices, body(): lax.all_to_all(arrived4, 'dp', split_axis=3, concat_axis=1, tiled=True)  240 us
    all_to_all x1, waiting for transfers between devices, body(): lax.all_to_all(grad_in4, 'dp', split_axis=3, concat_axis=1, tiled=True)  185 us
    all_to_all x1, blocking collectives, body(): lax.all_to_all(send, 'expert', split_axis=1, concat_axis=1, tiled=True)  59.9 us
    psum x1, waiting for transfers between devices, body(): lax.psum(jnp.dot(tokens.T, logit_grad, preferred_element_type=f32), ('exp...  53.9 us
    all_to_all x1, waiting for transfers between devices, body(): lax.all_to_all(grad_send, 'expert', split_axis=1, concat_axis=1, tiled=True)  43.1 us
    all_to_all x1, waiting for transfers between devices, body(): lax.all_to_all(input_grad, 'expert', split_axis=1, concat_axis=1, tiled=T...  42.3 us
    all_to_all x1, waiting for transfers between devices, body(): lax.all_to_all(expert_out, 'expert', split_axis=1, concat_axis=1, tiled=T...  40.4 us
  transfers between devices with their start and end apart: 9, of which 6 were waited for; matrix products, arithmetic and copies ran while one was open for 20% of the time, Pallas kernels for 0%

commit v1 on v0

--- a/solution.py
+++ b/solution.py
@@ -2,6 +2,7 @@
 import jax.numpy as jnp
 from jax import lax
 from jax.sharding import PartitionSpec as P
+from jax.lax import all_gather
 
 
 def flat_rows(array):
@@ -82,9 +83,8 @@
     pick = (expert_ids[:, :, None] == ladder[None, None, :]).astype(f32)
     logit_grad = jnp.einsum("tk,tke->te", sel_grad, pick).astype(bf16)
     token_grad = (moe_grad + jnp.dot(logit_grad, router.T, preferred_element_type=f32)).astype(bf16)
-    router_grad = lax.psum(
-        jnp.dot(tokens.T, logit_grad, preferred_element_type=f32), ("expert", "dp")
-    )
+    row_data = jnp.dot(tokens.T, logit_grad, preferred_element_type=f32)
+    router_grad = jnp.sum(all_gather(row_data, ("expert", "dp")), axis=0)
     hidden_width = hidden.shape[2]
     arrived4 = results[2]
     columns = (

time: 946 us -> 1010 us (1.068)
  waiting for transfers between devices: 606 us -> 664 us
    all_to_all x1, waiting for transfers between devices: 240 us -> 295 us  [body(): lax.all_to_all(arrived4, 'dp', split_axis=3, concat_axis=1, tiled=True)]
    psum x1 -> x0, waiting for transfers between devices: 53.9 us -> none  [body(): lax.psum(jnp.dot(tokens.T, logit_grad, preferred_element_type=f32), ('exp...]
    all_to_all x1, waiting for transfers between devices: 185 us -> 224 us  [body(): lax.all_to_all(grad_in4, 'dp', split_axis=3, concat_axis=1, tiled=True)]
    all_to_all x1, waiting for transfers between devices: 43.1 us -> 54.1 us  [body(): lax.all_to_all(grad_send, 'expert', split_axis=1, concat_axis=1, tiled=True)]
  transfers between devices with their start and end apart: 9 -> 9, of which waited for: 6 -> 5; matrix products, arithmetic and copies ran while one was open for 20% -> 16% of each run, Pallas kernels for 0% -> 0%
where the time goes in v1:
time: 1010 us; the launch traced here: 998 us
  waiting for transfers between devices  664 us (66%)
  local copies, waits for them, and re-layouts  135 us (13%)
  matrix products  79.1 us (8%)
  blocking collectives  59.9 us (6%)
  starting transfers between devices  27.5 us (3%)
  other arithmetic  18.2 us (2%)
  between operations  14.4 us (1%)
    all_to_all x1, waiting for transfers between devices, body(): lax.all_to_all(arrived4, 'dp', split_axis=3, concat_axis=1, tiled=True)  295 us
    all_to_all x1, waiting for transfers between devices, body(): lax.all_to_all(grad_in4, 'dp', split_axis=3, concat_axis=1, tiled=True)  224 us
    all_to_all x1, blocking collectives, body(): lax.all_to_all(send, 'expert', split_axis=1, concat_axis=1, tiled=True)  59.9 us
    all_to_all x1, waiting for transfers between devices, body(): lax.all_to_all(grad_send, 'expert', split_axis=1, concat_axis=1, tiled=True)  54.1 us
    all_to_all x1, waiting for transfers between devices, body(): lax.all_to_all(expert_out, 'expert', split_axis=1, concat_axis=1, tiled=T...  46.8 us
    all_to_all x1, waiting for transfers between devices, body(): lax.all_to_all(input_grad, 'expert', split_axis=1, concat_axis=1, tiled=T...  43.1 us
  transfers between devices with their start and end apart: 9, of which 5 were waited for; matrix products, arithmetic and copies ran while one was open for 16% of the time, Pallas kernels for 0%

profile of v1, /device:TPU:0, one launch (start us, length us, event | category | flops | bytes accessed | tf_op | source)
XLA Modules:
  0.0 998.0 jit_solution(15425907123020387887)
XLA Ops:
  7.2 0.9 copy.108
  8.4 4.5 reduce-window.6
  13.0 0.1 copy.111
  13.4 4.3 scatter_custom_fusion
  17.9 6.0 gather_fusion
  23.9 2.7 copy_select_fusion
  26.6 59.9 %all_to_all.50 = bf16[2,8,72,2048]{3,2,0,1:T(8,128)(2,1)S(1)} all-to-all(bf16[2,8,72,2048]{3,2,0,1:T(8,128)(2,1)S(1)} %copy_select_fusion), channel_id=1, replica_groups=mesh['expert'=8,'dp'=4] {'expert'}, dimensions={1} | all-to-all | bytes 9437184 | tf_op jit(solution)/shard_map/all_to_all | solution.py:41
  86.5 0.7 copy.115
  87.2 1.7 copy-done.3
  88.9 3.8 fusion.33
  92.8 5.6 multiply_convert_fusion.2
  98.4 4.1 convolution_convert_fusion
  102.5 2.6 copy.116
  105.1 4.8 all-to-all-start.1
  109.9 0.2 all-gather.12.cloned.1.call-start
  110.1 0.1 copy.106
  110.3 0.2 fusion.10
  110.6 7.0 gather_fusion.5
  117.8 46.8 %all-to-all-done.1 = bf16[2,8,72,2048]{3,2,0,1:T(8,128)(2,1)} async-done(((bf16[2,8,72,2048]{3,2,0,1:T(8,128)(2,1)}), bf16[2,8,72,2048]{3,2,0,1:T(8,128)(2,1)}, u32[]{:S(2)}, u32[]{:S(2)}) %all-to-all-start.1) | async-done | bytes 4718624 | tf_op jit(solution)/shard_map/all_to_all | solution.py:54
  164.6 5.3 copy.117
  169.9 11.7 %gather_fusion.1 = bf16[1024,2048]{1,0:T(8,128)(2,1)} fusion(bf16[1152,2048]{1,0:T(8,128)(2,1)} %bitcast.109, s32[1024]{0:T(1024)S(1)} %broadcast_clamp_fusion), kind=kCustom, calls=%fused_computation.1 | custom fusion | bytes 8392704 | tf_op jit(solution)/shard_map/gather | solution.py:57
  181.6 4.9 fusion.2
  186.6 0.1 copy.137
  186.8 0.3 fusion.12
  187.1 0.9 convolution_bitcast_fusion
  188.1 0.7 all-gather.10.cloned.1.call-update
  188.8 6.0 gather_fusion.3
  194.7 0.1 copy.118
  194.9 4.6 gather_fusion.2
  199.6 4.4 fusion.1
  204.0 4.6 all-to-all-start.2
  208.6 11.7 %copy.125 = bf16[2,8,72,2048]{2,1,0,3:T(8,128)(2,1)} copy(bf16[2,8,72,2048]{3,2,0,1:T(8,128)(2,1)} %copy-done.3) | data formatting | bytes 9437184 | tf_op jit(solution)/shard_map/all_to_all | solution.py:41
  220.3 54.1 %all-to-all-done.2 = bf16[2,8,72,2048]{3,2,0,1:T(8,128)(2,1)} async-done(((bf16[2,8,72,2048]{3,2,0,1:T(8,128)(2,1)}), bf16[2,8,72,2048]{3,2,0,1:T(8,128)(2,1)}, u32[]{:S(2)}, u32[]{:S(2)}) %all-to-all-start.2) | async-done | bytes 4718624 | tf_op jit(solution)/shard_map/all_to_all | solution.py:63
  274.4 5.6 all-to-all-start.4
  280.1 2.9 copy.121
  283.0 0.4 copy-done.9
  283.4 0.9 copy-done.10
  284.3 9.1 multiply_convert_fusion
  293.4 10.9 %fusion.34 = f32[2,576,2048]{2,1,0:T(8,128)} fusion(bf16[2,576,640]{2,1,0:T(8,128)(2,1)} %get-tuple-element.11, bf16[2,2048,640]{2,1,0:T(8,128)(2,1)} %param.10), kind=kOutput, calls=%fused_computation.87 | convolution fusion | flops 3019898880 | bytes 16154624 | tf_op jit(solution)/shard_map/jrf,jdf->jrd/dot_general | solution.py:73
  304.3 8.1 add_convert_fusion
  312.4 2.5 copy.122
  314.9 294.9 %all-to-all-done.4 = bf16[2,8,72,2048]{2,1,0,3:T(8,128)(2,1)} async-done(((bf16[2,8,72,2048]{2,1,0,3:T(8,128)(2,1)}), bf16[2,8,72,2048]{2,1,0,3:T(8,128)(2,1)}, u32[]{:S(2)}, u32[]{:S(2)}) %all-to-all-start.4) | async-done | bytes 4718624 | tf_op jit(solution)/shard_map/all_to_all | solution.py:91
  609.9 4.6 all-to-all-start.3
  614.5 11.7 %copy.130 = bf16[2,8,72,2048]{2,1,0,3:T(8,128)(2,1)} copy(bf16[2,8,72,2048]{3,2,0,1:T(8,128)(2,1)} %all-to-all-done.2) | data formatting | bytes 9437184 | tf_op jit(solution)/shard_map/all_to_all | solution.py:63
  626.1 43.1 %all-to-all-done.3 = bf16[2,8,72,2048]{3,2,0,1:T(8,128)(2,1)} async-done(((bf16[2,8,72,2048]{3,2,0,1:T(8,128)(2,1)}), bf16[2,8,72,2048]{3,2,0,1:T(8,128)(2,1)}, u32[]{:S(2)}, u32[]{:S(2)}) %all-to-all-start.3) | async-done | bytes 4718624 | tf_op jit(solution)/shard_map/all_to_all | solution.py:77
  669.2 7.2 all-to-all-start.5
  676.4 0.4 all-gather.8.cloned.1.call-start
  676.8 0.1 all-gather.8.cloned.1.call-update
  677.0 0.1 copy.133
  677.1 3.4 fusion.4
  680.5 1.1 copy.155
  681.6 10.9 %copy.142 = bf16[2,8,72,4,512]{4,3,2,1,0:T(4,128)(2,1)} copy(bf16[2,8,72,4,512]{2,1,0,4,3:T(8,128)(2,1)} %bitcast.23) | data formatting | bytes 9437184 | tf_op jit(solution)/shard_map/all_to_all | solution.py:91
  692.5 5.4 copy.127
  698.0 4.6 copy.144
  702.6 1.2 bitcast_reduce_fusion
  703.7 5.3 copy.123
  709.0 11.8 %gather_fusion.4 = bf16[1024,2048]{1,0:T(8,128)(2,1)} fusion(bf16[1152,2048]{1,0:T(8,128)(2,1)} %bitcast.108, s32[1024]{0:T(1024)S(1)} %broadcast_clamp_fusion), kind=kCustom, calls=%fused_computation.4 | custom fusion | bytes 8392704 | tf_op jit(solution)/shard_map/gather | solution.py:80
  720.8 5.1 convert_reduce_fusion
  725.9 1.1 fusion.7
  727.0 224.4 %all-to-all-done.5 = bf16[2,8,72,2048]{2,1,0,3:T(8,128)(2,1)} async-done(((bf16[2,8,72,2048]{2,1,0,3:T(8,128)(2,1)}), bf16[2,8,72,2048]{2,1,0,3:T(8,128)(2,1)}, u32[]{:S(2)}, u32[]{:S(2)}) %all-to-all-start.5) | async-done | bytes 4718624 | tf_op jit(solution)/shard_map/all_to_all | solution.py:92
  951.4 13.2 %copy.131 = bf16[2,8,72,4,512]{4,2,1,3,0:T(8,128)(2,1)} copy(bf16[2,8,72,4,512]{2,1,0,4,3:T(8,128)(2,1)} %bitcast.32) | data formatting | bytes 9437184 | tf_op jit(solution)/shard_map/all_to_all | solution.py:92
  964.6 8.4 convolution_convert_fusion.1
  973.0 9.1 convolution_convert_fusion.3
  982.1 9.1 convolution_convert_fusion.2
  (71 shorter events, 1.5 us)
Async XLA Ops:
  7.2 174.5 %copy-start = (bf16[128,2048]{1,0:T(8,128)(2,1)S(1)}, bf16[128,2048]{1,0:T(8,128)(2,1)}, u32[]{:S(2)}) copy-start(bf16[128,2048]{1,0:T(8,128)(2,1)} %param.13) | copy-start | bytes 1572868
  7.2 10.7 %copy-start.2 = (bf16[128,2048]{1,0:T(8,128)(2,1)S(1)}, bf16[128,2048]{1,0:T(8,128)(2,1)}, u32[]{:S(2)}) copy-start(bf16[128,2048]{1,0:T(8,128)(2,1)} %param.7) | copy-start | bytes 1572868
  26.6 62.3 %slice-start.2 = ((s8[5242880]{0:T(1024)(128)(4,1)}), s8[4194304]{0:T(1024)(128)(4,1)S(1)}, s32[]{:S(2)}) async-start(s8[5242880]{0:T(1024)(128)(4,1)} %bitcast.139), calls=%async_computation.12 | async-start | bytes 8388608
  86.5 2.4 copy-start.3
  86.5 2.4 slice-start.3
  86.5 6.3 slice-start.4
  88.9 3.9 slice-start.5
  88.9 9.5 slice-start
  92.8 5.6 copy-start.8
  92.8 5.6 slice-start.1
  98.4 4.1 copy-start.4
  105.1 5.0 copy-start.7
  105.1 5.2 copy-start.6
  105.1 59.5 %all-to-all-start.1 = ((bf16[2,8,72,2048]{3,2,0,1:T(8,128)(2,1)}), bf16[2,8,72,2048]{3,2,0,1:T(8,128)(2,1)}, u32[]{:S(2)}, u32[]{:S(2)}) async-start(bf16[2,8,72,2048]{3,2,0,1:T(8,128)(2,1)} %copy.116), calls=%async_computation.1 | async-start | bytes 9437184 | tf_op jit(solution)/shard_map/all_to_all | solution.py:54
  109.9 588.1 %all-gather.12.cloned.1.call-start = ((), (), s32[]{:S(2)}) async-start(), calls=%async_computation.9 | async-start | bytes 4325376 | tf_op jit(solution)/shard_map/all_gather | solution.py:87
  188.0 776.6 %all-gather.10.cloned.1.call-start = ((), (), s32[]{:S(2)}) async-start(), calls=%async_computation.8 | async-start | bytes 7372800 | tf_op jit(solution)/shard_map/all_gather | solution.py:98
  204.0 70.4 %all-to-all-start.2 = ((bf16[2,8,72,2048]{3,2,0,1:T(8,128)(2,1)}), bf16[2,8,72,2048]{3,2,0,1:T(8,128)(2,1)}, u32[]{:S(2)}, u32[]{:S(2)}) async-start(bf16[2,8,72,2048]{3,2,0,1:T(8,128)(2,1)} %fusion.1), calls=%async_computation.2 | async-start | bytes 9437184 | tf_op jit(solution)/shard_map/all_to_all | solution.py:63
  274.4 335.4 %all-to-all-start.4 = ((bf16[2,8,72,2048]{2,1,0,3:T(8,128)(2,1)}), bf16[2,8,72,2048]{2,1,0,3:T(8,128)(2,1)}, u32[]{:S(2)}, u32[]{:S(2)}) async-start(bf16[2,8,72,2048]{2,1,0,3:T(8,128)(2,1)} %copy.125), calls=%async_computation.4 | async-start | bytes 16777216 | tf_op jit(solution)/shard_map/all_to_all | solution.py:91
  280.1 692.9 %all-gather.6.cloned.1.call-start = ((), (), s32[]{:S(2)}) async-start(), calls=%async_computation.6 | async-start | bytes 7372800 | tf_op jit(solution)/shard_map/all_gather | solution.py:96
  280.1 3.3 copy-start.9
  280.1 4.2 copy-start.10
  293.4 11.0 %copy-start.5 = (bf16[2,576,640]{2,1,0:T(8,128)(2,1)}, bf16[2,576,640]{2,1,0:T(8,128)(2,1)S(1)}, u32[]{:S(2)}) copy-start(bf16[2,576,640]{2,1,0:T(8,128)(2,1)S(1)} %get-tuple-element.10) | copy-start | bytes 4423684
  609.9 59.3 %all-to-all-start.3 = ((bf16[2,8,72,2048]{3,2,0,1:T(8,128)(2,1)}), bf16[2,8,72,2048]{3,2,0,1:T(8,128)(2,1)}, u32[]{:S(2)}, u32[]{:S(2)}) async-start(bf16[2,8,72,2048]{3,2,0,1:T(8,128)(2,1)} %copy.122), calls=%async_computation.3 | async-start | bytes 9437184 | tf_op jit(solution)/shard_map/all_to_all | solution.py:77
  669.2 282.2 %all-to-all-start.5 = ((bf16[2,8,72,2048]{2,1,0,3:T(8,128)(2,1)}), bf16[2,8,72,2048]{2,1,0,3:T(8,128)(2,1)}, u32[]{:S(2)}, u32[]{:S(2)}) async-start(bf16[2,8,72,2048]{2,1,0,3:T(8,128)(2,1)} %copy.130), calls=%async_computation.5 | async-start | bytes 16777216 | tf_op jit(solution)/shard_map/all_to_all | solution.py:92
  676.4 305.7 %all-gather.8.cloned.1.call-start = ((), (), s32[]{:S(2)}) async-start(), calls=%async_computation.7 | async-start | bytes 7372800 | tf_op jit(solution)/shard_map/all_gather | solution.py:97
  982.1 9.1 copy-start.1
Sparse Core Ops, SparseCore 0:
  188.1 78.8 all-gather.11
  268.6 245.4 all-gather.9
  515.7 135.0 all-gather.5
  678.5 232.6 all-gather.7
